TPU v7x, 32 devices: a whole 2x2x4 slice. The times are simulated.
32 devices in a mesh: dp: 4 (over y, core), mp: 8 (over z, x).
Axes of the slice: x: 2, y: 2, z: 4, core: 2. Of those that a mesh axis runs over, the one named last changes fastest.
Arguments:
- features: bfloat16 [8, 24, 24, 1024], P('dp'), may hold values from -6 to 6
- w_in: bfloat16 [2, 1024, 1024], P(None, 'mp'), may hold values from -0.1875 to 0.1875
- ln_gain: float32 [2, 1024], P(None, 'mp'), may hold values from 0.5 to 1.5
- ln_bias: float32 [2, 1024], P(None, 'mp'), may hold values from -3 to 3
- w_conv: bfloat16 [2, 1024, 9, 1024], P(None, 'mp')
- se_down: bfloat16 [2, 1024, 256], P(None, 'mp'), may hold values from -0.375 to 0.375
- se_down_bias: float32 [2, 256], replicated, may hold values from -3 to 3
- se_up: bfloat16 [2, 256, 1024], P(None, None, 'mp'), may hold values from -0.375 to 0.375
- se_up_bias: float32 [2, 1024], P(None, 'mp'), may hold values from -3 to 3
- w_out: bfloat16 [2, 1024, 1024], P(None, 'mp'), may hold values from -0.375 to 0.375
- w_read1: bfloat16 [1024, 4096], P(None, 'mp'), may hold values from -0.1875 to 0.1875
- b_read1: float32 [4096], P('mp'), may hold values from -3 to 3
- w_read2: bfloat16 [4096, 4096], P('mp'), may hold values from -0.09375 to 0.09375
- b_read2: float32 [4096], P('mp'), may hold values from -3 to 3
- out_grad: bfloat16 [8, 12, 12, 4096], P('dp', None, None, 'mp'), may hold values from -6 to 6
- box_counts: int32 [8], P('dp'), may hold values from 1 to 4
Outputs:
- readout: bfloat16 [8, 12, 12, 4096], P('dp', None, None, 'mp')
- grad_features: float32 [8, 24, 24, 1024], P('dp', None, None, 'mp')
- grad_w_in: float32 [2, 1024, 1024], P(None, 'mp', 'dp')
- grad_ln_gain: float32 [2, 1024], P(None, 'mp')
- grad_ln_bias: float32 [2, 1024], P(None, 'mp')
- grad_w_conv: float32 [2, 1024, 9, 1024], P(None, 'mp', None, 'dp')
- grad_se_down: float32 [2, 1024, 256], P(None, 'mp', 'dp')
- grad_se_down_bias: float32 [2, 256], replicated
- grad_se_up: float32 [2, 256, 1024], P(None, 'dp', 'mp')
- grad_se_up_bias: float32 [2, 1024], P(None, 'mp')
- grad_w_out: float32 [2, 1024, 1024], P(None, 'mp', 'dp')
- grad_w_read1: float32 [1024, 4096], P('dp', 'mp')
- grad_b_read1: float32 [4096], P('mp')
- grad_w_read2: float32 [4096, 4096], P('mp', 'dp')
- grad_b_read2: float32 [4096], P('mp')
All inputs are finite; a program needn't handle non-finite values.
Results may differ from a plain program's by a relative error of at most 0.017.
Values may be sent and summed in bfloat16 or wider, within the bound.
A program may use at most 128 MiB of HBM per device.

v0:
```python
from functools import partial

import jax
import jax.numpy as jnp
from jax import lax
from jax.sharding import PartitionSpec as P

epsilon = 1e-06
highest = lax.Precision.HIGHEST


def all_channels(value):
    return lax.all_gather(value, "mp", axis=3, tiled=True)


def channel_share(value):
    return lax.psum_scatter(value, "mp", scatter_dimension=3, tiled=True)


def channel_total(value):
    return lax.psum(value, "mp")


def project(left, weight):
    return jnp.einsum("bijc,cd->bijd", left, weight, preferred_element_type=jnp.float32)


def project_t(left, weight):
    return jnp.einsum("bijc,dc->bijd", left, weight, preferred_element_type=jnp.float32)


def weight_grad(left, right):
    return jnp.einsum("bijc,bijd->cd", left, right, preferred_element_type=jnp.float32)


def pad_grid(value):
    return jnp.pad(value, ((0, 0), (1, 1), (1, 1), (0, 0)))


def window(padded, start_down, start_right, grid_side):
    return padded[:, start_down : start_down + grid_side, start_right : start_right + grid_side, :]


def conv_forward(full_in, w_conv):
    grid_side = full_in.shape[1]
    padded = pad_grid(full_in)
    result = jnp.zeros(full_in.shape[:3] + (w_conv.shape[0],), jnp.float32)
    for offset in range(9):
        result = result + project_t(
            window(padded, offset // 3, offset % 3, grid_side), w_conv[:, offset, :]
        )
    return result


def conv_backward(grad_conv, w_conv):
    grid_side = grad_conv.shape[1]
    padded = pad_grid(grad_conv)
    result = jnp.zeros(grad_conv.shape[:3] + (w_conv.shape[2],), jnp.float32)
    for offset in range(9):
        result = result + project(
            window(padded, 2 - offset // 3, 2 - offset % 3, grid_side), w_conv[:, offset, :]
        )
    return channel_share(result)


def back_project(grad_low, weight):
    return channel_share(project(grad_low, weight))


def block_forward(in_low, in_full, value, weights):
    w_in, gain, shift, w_conv, se_down, se_down_bias, se_up, se_up_bias, w_out = weights
    reduced = project_t(in_full, w_in)
    full_width = in_full.shape[3]
    row_total, row_squares = channel_total(
        (jnp.sum(reduced, axis=3, keepdims=True), jnp.sum(reduced * reduced, axis=3, keepdims=True))
    )
    row_mean = row_total / full_width
    inv_std = lax.rsqrt(row_squares / full_width - row_mean * row_mean + epsilon)
    normed = (reduced - row_mean) * inv_std
    norm_low = (normed * gain + shift).astype(jnp.bfloat16)
    norm_full = all_channels(norm_low)
    conv_out = conv_forward(norm_full, w_conv)
    activated = jax.nn.silu(conv_out)
    pooled = jnp.mean(activated, axis=(1, 2))
    pre_down = (
        channel_total(jnp.dot(pooled, se_down.astype(jnp.float32), precision=highest))
        + se_down_bias
    )
    squeeze = jax.nn.silu(pre_down)
    excite = jax.nn.sigmoid(
        jnp.dot(squeeze, se_up.astype(jnp.float32), precision=highest) + se_up_bias
    )
    scale_low = (activated * excite[:, None, None, :]).astype(jnp.bfloat16)
    scale_full = all_channels(scale_low)
    result = value + project_t(scale_full, w_out)
    stored = (
        in_low,
        in_full,
        normed,
        inv_std,
        norm_low,
        norm_full,
        conv_out,
        activated,
        pooled,
        pre_down,
        squeeze,
        excite,
        scale_low,
        scale_full,
    )
    return (result, stored)


def block_backward(grad_out, stored, weights):
    (
        in_low,
        in_full,
        normed,
        inv_std,
        norm_low,
        norm_full,
        conv_out,
        activated,
        pooled,
        pre_down,
        squeeze,
        excite,
        scale_low,
        scale_full,
    ) = stored
    w_in, gain, shift, w_conv, se_down, se_down_bias, se_up, se_up_bias, w_out = weights
    grid_side = activated.shape[1]
    full_width = in_full.shape[3]
    grad_y = grad_out.astype(jnp.bfloat16)
    grad_w_out = weight_grad(grad_y, scale_full)
    grad_scaled = back_project(grad_y, w_out)
    gate_grad = jnp.sum(grad_scaled * activated, axis=(1, 2))
    grad_up = gate_grad * excite * (1.0 - excite)
    grad_up_bias = jnp.sum(grad_up, axis=0)
    grad_se_up = jnp.dot(squeeze.T, grad_up, precision=highest)
    grad_squeeze = channel_total(jnp.dot(grad_up, se_up.astype(jnp.float32).T, precision=highest))
    ignored, squeeze_back = jax.vjp(jax.nn.silu, pre_down)
    grad_down = squeeze_back(grad_squeeze)[0]
    grad_down_bias = jnp.sum(grad_down, axis=0)
    grad_se_down = jnp.dot(pooled.T, grad_down, precision=highest)
    grad_pooled = jnp.dot(grad_down, se_down.astype(jnp.float32).T, precision=highest)
    grad_act = grad_scaled * excite[:, None, None, :] + grad_pooled[:, None, None, :] / (
        grid_side * grid_side
    )
    ignored, act_back = jax.vjp(jax.nn.silu, conv_out)
    grad_conv = act_back(grad_act)[0].astype(jnp.bfloat16)
    padded = pad_grid(norm_full)
    grad_w_conv = jnp.stack(
        [
            weight_grad(grad_conv, window(padded, offset // 3, offset % 3, grid_side))
            for offset in range(9)
        ],
        axis=1,
    )
    grad_norm = conv_backward(grad_conv, w_conv)
    grad_gain = jnp.sum(grad_norm * normed, axis=(0, 1, 2))
    grad_shift = jnp.sum(grad_norm, axis=(0, 1, 2))
    grad_hat = grad_norm * gain
    first_sum, second_sum = channel_total(
        (
            jnp.sum(grad_hat, axis=3, keepdims=True),
            jnp.sum(grad_hat * normed, axis=3, keepdims=True),
        )
    )
    grad_reduced = (
        inv_std * (grad_hat - first_sum / full_width - normed * second_sum / full_width)
    ).astype(jnp.bfloat16)
    grad_w_in = weight_grad(grad_reduced, in_full)
    grad_in = grad_out + back_project(grad_reduced, w_in)
    return (
        grad_in,
        (
            grad_w_in,
            grad_gain,
            grad_shift,
            grad_w_conv,
            grad_se_down,
            grad_down_bias,
            grad_se_up,
            grad_up_bias,
            grad_w_out,
        ),
    )


def on_device(
    features,
    w_in,
    ln_gain,
    ln_bias,
    w_conv,
    se_down,
    se_down_bias,
    se_up,
    se_up_bias,
    w_out,
    w_read1,
    b_read1,
    w_read2,
    b_read2,
    out_grad,
    box_counts,
):

    def weights_of(index):
        return (
            w_in[index],
            ln_gain[index],
            ln_bias[index],
            w_conv[index],
            se_down[index],
            se_down_bias[index],
            se_up[index],
            se_up_bias[index],
            w_out[index],
        )

    local_width = w_in.shape[1]
    row_start = lax.axis_index("mp") * local_width
    own_features = lax.dynamic_slice_in_dim(features, row_start, local_width, 3).astype(jnp.float32)
    first_out, first_stored = block_forward(None, features, own_features, weights_of(0))
    shape = first_out.shape
    pooled_in = jnp.mean(
        first_out.reshape(shape[0], shape[1] // 2, 2, shape[2] // 2, 2, shape[3]), axis=(2, 4)
    )
    pooled_low = pooled_in.astype(jnp.bfloat16)
    second_out, second_stored = block_forward(
        pooled_low, all_channels(pooled_low), pooled_in, weights_of(1)
    )
    top_low = second_out.astype(jnp.bfloat16)
    top_full = all_channels(top_low)
    hidden_pre = project(top_full, w_read1) + b_read1
    hidden_act, gelu_back = jax.vjp(partial(jax.nn.gelu, approximate=False), hidden_pre)
    act_low = hidden_act.astype(jnp.bfloat16)
    result = channel_share(project(act_low, w_read2)) + b_read2
    readout = result.astype(jnp.bfloat16)
    grad_top = (
        out_grad.astype(jnp.float32) * box_counts.astype(jnp.float32)[:, None, None, None]
    ).astype(jnp.bfloat16)
    grad_b_read2 = jnp.sum(grad_top.astype(jnp.float32), axis=(0, 1, 2))
    grad_full = all_channels(grad_top)
    grad_w_read2 = weight_grad(act_low, grad_full)
    grad_hidden = project_t(grad_full, w_read2)
    grad_pre = gelu_back(grad_hidden)[0].astype(jnp.bfloat16)
    grad_b_read1 = jnp.sum(grad_pre.astype(jnp.float32), axis=(0, 1, 2))
    grad_w_read1 = weight_grad(top_full, grad_pre)
    grad_second = channel_share(project_t(grad_pre, w_read1))
    grad_pool, second_grads = block_backward(grad_second, second_stored, weights_of(1))
    grad_first = jnp.repeat(jnp.repeat(grad_pool, 2, axis=1), 2, axis=2) * 0.25
    grad_features, first_grads = block_backward(grad_first, first_stored, weights_of(0))
    stacked = [
        jnp.stack([first_part, second_part])
        for first_part, second_part in zip(first_grads, second_grads)
    ]
    matrices = (
        lax.psum_scatter(stacked[0], "dp", scatter_dimension=2, tiled=True),
        lax.psum_scatter(stacked[3], "dp", scatter_dimension=3, tiled=True),
        lax.psum_scatter(stacked[4], "dp", scatter_dimension=2, tiled=True),
        lax.psum_scatter(stacked[6], "dp", scatter_dimension=1, tiled=True),
        lax.psum_scatter(stacked[8], "dp", scatter_dimension=2, tiled=True),
        lax.psum_scatter(grad_w_read1, "dp", scatter_dimension=0, tiled=True),
        lax.psum_scatter(grad_w_read2, "dp", scatter_dimension=1, tiled=True),
    )
    vectors = lax.psum(
        (stacked[1], stacked[2], stacked[5], stacked[7], grad_b_read1, grad_b_read2), "dp"
    )
    return (
        readout,
        grad_features,
        matrices[0],
        vectors[0],
        vectors[1],
        matrices[1],
        matrices[2],
        vectors[2],
        matrices[3],
        vectors[3],
        matrices[4],
        matrices[5],
        vectors[4],
        matrices[6],
        vectors[5],
    )


def solution(mesh):
    in_specs = (
        P("dp", None, None, None),
        P(None, "mp", None),
        P(None, "mp"),
        P(None, "mp"),
        P(None, "mp", None, None),
        P(None, "mp", None),
        P(),
        P(None, None, "mp"),
        P(None, "mp"),
        P(None, "mp", None),
        P(None, "mp"),
        P("mp"),
        P("mp", None),
        P("mp"),
        P("dp", None, None, "mp"),
        P("dp"),
    )
    out_specs = (
        P("dp", None, None, "mp"),
        P("dp", None, None, "mp"),
        P(None, "mp", "dp"),
        P(None, "mp"),
        P(None, "mp"),
        P(None, "mp", None, "dp"),
        P(None, "mp", "dp"),
        P(),
        P(None, "dp", "mp"),
        P(None, "mp"),
        P(None, "mp", "dp"),
        P("dp", "mp"),
        P("mp"),
        P("mp", "dp"),
        P("mp"),
    )
    return jax.shard_map(
        on_device, mesh=mesh, in_specs=in_specs, out_specs=out_specs, check_vma=False
    )
```

profile of v0, /device:TPU:0, one launch (start us, length us, event | category | flops | bytes accessed | tf_op | source)
XLA Modules:
  0.0 1517.8 jit_solution(13126324462275967476)
XLA Ops:
  9.9 39.3 %all-reduce.8 = (f32[2,24,24,1]{2,1,0,3:T(8,128)S(1)}, f32[2,24,24,1]{2,1,0,3:T(8,128)S(1)}) all-reduce(f32[2,24,24,1]{2,1,0,3:T(8,128)S(1)} %bitcast.525, f32[2,24,24,1]{2,1,0,3:T(8,128)S(1)} %bitcast.524), channel_id=1, replica_groups=mesh['dp'=4,'mp'=8] {'mp'}, use_global_device_ids=true, to_apply=%region_3.0 | all-reduce | flops 2304 | bytes 18432 | tf_op jit(solution)/shard_map/psum | solution.py:21
  57.4 44.8 %all-gather.4.cloned.1.call-done = bf16[2,24,24,1024]{3,2,1,0:T(8,128)(2,1)} async-done(((bf16[2,24,24,128]{3,2,1,0:T(8,128)(2,1)}), bf16[2,24,24,1024]{3,2,1,0:T(8,128)(2,1)}) %all-gather.4.cloned.1.call-update) | async-done | bytes 2359312 | tf_op jit(solution)/shard_map/all_gather | solution.py:13
  115.0 18.5 %psum.128 = f32[2,256]{1,0:T(2,128)S(1)} all-reduce(f32[2,256]{1,0:T(2,128)S(1)} %fusion.183), channel_id=1, replica_groups=mesh['dp'=4,'mp'=8] {'mp'}, use_global_device_ids=true, to_apply=%region_5.6 | all-reduce | flops 512 | bytes 4096 | tf_op jit(solution)/shard_map/psum | solution.py:21
  140.6 47.7 %all-gather.6.cloned.1.call-done = bf16[2,24,24,1024]{3,2,1,0:T(8,128)(2,1)} async-done(((bf16[2,24,24,128]{3,2,1,0:T(8,128)(2,1)}), bf16[2,24,24,1024]{3,2,1,0:T(8,128)(2,1)}) %all-gather.6.cloned.1.call-update) | async-done | bytes 2359312 | tf_op jit(solution)/shard_map/all_gather | solution.py:13
  194.7 32.9 %all_gather.23 = bf16[2,12,12,1024]{3,2,1,0:T(8,128)(2,1)S(1)} all-gather(bf16[2,12,12,128]{3,2,1,0:T(8,128)(2,1)S(1)} %multiply_convert_fusion.6), channel_id=1, replica_groups=mesh['dp'=4,'mp'=8] {'mp'}, dimensions={3}, use_global_device_ids=true | all-gather | bytes 663552 | tf_op jit(solution)/shard_map/all_gather | solution.py:13
  231.1 36.0 %all-reduce.7 = (f32[2,12,12,1]{2,1,0,3:T(8,128)}, f32[2,12,12,1]{2,1,0,3:T(8,128)}) all-reduce(f32[2,12,12,1]{2,1,0,3:T(8,128)} %bitcast.522, f32[2,12,12,1]{2,1,0,3:T(8,128)S(1)} %bitcast.521), channel_id=1, replica_groups=mesh['dp'=4,'mp'=8] {'mp'}, use_global_device_ids=true, to_apply=%region_10.11 | all-reduce | flops 576 | bytes 4608 | tf_op jit(solution)/shard_map/psum | solution.py:21
  269.1 28.6 %all_gather.24 = bf16[2,12,12,1024]{3,2,1,0:T(8,128)(2,1)S(1)} all-gather(bf16[2,12,12,128]{3,2,1,0:T(8,128)(2,1)S(1)} %add_convert_fusion.3), channel_id=1, replica_groups=mesh['dp'=4,'mp'=8] {'mp'}, dimensions={3}, use_global_device_ids=true | all-gather | bytes 663552 | tf_op jit(solution)/shard_map/all_gather | solution.py:13
  304.3 18.2 %psum.131 = f32[2,256]{1,0:T(2,128)} all-reduce(f32[2,256]{1,0:T(2,128)} %fusion.177), channel_id=1, replica_groups=mesh['dp'=4,'mp'=8] {'mp'}, use_global_device_ids=true, to_apply=%region_12.13 | all-reduce | flops 512 | bytes 4096 | tf_op jit(solution)/shard_map/psum | solution.py:21
  324.6 28.9 %all_gather.25 = bf16[2,12,12,1024]{3,2,1,0:T(8,128)(2,1)S(1)} all-gather(bf16[2,12,12,128]{3,2,1,0:T(8,128)(2,1)S(1)} %multiply_convert_fusion.5), channel_id=1, replica_groups=mesh['dp'=4,'mp'=8] {'mp'}, dimensions={3}, use_global_device_ids=true | all-gather | bytes 663552 | tf_op jit(solution)/shard_map/all_gather | solution.py:13
  355.8 27.7 %all_gather.26 = bf16[2,12,12,1024]{3,2,1,0:T(8,128)(2,1)S(1)} all-gather(bf16[2,12,12,128]{3,2,1,0:T(8,128)(2,1)S(1)} %fusion.54), channel_id=1, replica_groups=mesh['dp'=4,'mp'=8] {'mp'}, dimensions={3}, use_global_device_ids=true | all-gather | bytes 663552 | tf_op jit(solution)/shard_map/all_gather | solution.py:13
  396.7 62.7 %reduce-scatter.17.cloned.1.call-done = f32[2,12,12,128]{3,2,1,0:T(8,128)} async-done(((f32[2,12,12,1024]{3,2,1,0:T(8,128)}), f32[2,12,12,128]{3,2,1,0:T(8,128)}) %reduce-scatter.17.cloned.1.call-update) | async-done | bytes 147472 | tf_op jit(solution)/shard_map/reduce_scatter | solution.py:17
  462.1 66.2 %reduce-scatter.19.cloned.1.call-done = f32[2,12,12,128]{3,2,1,0:T(8,128)} async-done(((f32[2,12,12,1024]{3,2,1,0:T(8,128)}), f32[2,12,12,128]{3,2,1,0:T(8,128)}) %reduce-scatter.19.cloned.1.call-update) | async-done | bytes 147472 | tf_op jit(solution)/shard_map/reduce_scatter | solution.py:17
  529.8 31.5 %psum.132 = f32[2,256]{1,0:T(2,128)S(1)} all-reduce(f32[2,256]{1,0:T(2,128)S(1)} %fusion.173), channel_id=1, replica_groups=mesh['dp'=4,'mp'=8] {'mp'}, use_global_device_ids=true, to_apply=%region_17.18 | all-reduce | flops 512 | bytes 4096 | tf_op jit(solution)/shard_map/psum | solution.py:21
  568.9 63.0 %reduce-scatter.21.cloned.1.call-done = f32[2,12,12,128]{3,2,1,0:T(8,128)} async-done(((f32[2,12,12,1024]{3,2,1,0:T(8,128)}), f32[2,12,12,128]{3,2,1,0:T(8,128)}) %reduce-scatter.21.cloned.1.call-update) | async-done | bytes 147472 | tf_op jit(solution)/shard_map/reduce_scatter | solution.py:17
  633.8 35.1 %all-reduce.6 = (f32[2,12,12]{2,1,0:T(8,128)S(1)}, f32[2,12,12,1]{2,1,0,3:T(8,128)S(1)}) all-reduce(f32[2,12,12]{2,1,0:T(8,128)S(1)} %get-tuple-element.54, f32[2,12,12,1]{2,1,0,3:T(8,128)S(1)} %bitcast.523), channel_id=1, replica_groups=mesh['dp'=4,'mp'=8] {'mp'}, use_global_device_ids=true, to_apply=%region_22.23 | all-reduce | flops 576 | bytes 4608 | tf_op jit(solution)/shard_map/psum | solution.py:21
  672.7 63.0 %reduce-scatter.23.cloned.1.call-done = f32[2,12,12,128]{3,2,1,0:T(8,128)} async-done(((f32[2,12,12,1024]{3,2,1,0:T(8,128)}), f32[2,12,12,128]{3,2,1,0:T(8,128)}) %reduce-scatter.23.cloned.1.call-update) | async-done | bytes 147472 | tf_op jit(solution)/shard_map/reduce_scatter | solution.py:17
  740.6 94.7 %reduce-scatter.25.cloned.1.call-done = f32[2,24,24,128]{3,2,1,0:T(8,128)} async-done(((f32[2,24,24,1024]{3,2,1,0:T(8,128)}), f32[2,24,24,128]{3,2,1,0:T(8,128)}) %reduce-scatter.25.cloned.1.call-update) | async-done | bytes 589840 | tf_op jit(solution)/shard_map/reduce_scatter | solution.py:17
  837.0 20.2 %psum.135 = f32[2,256]{1,0:T(2,128)S(1)} all-reduce(f32[2,256]{1,0:T(2,128)S(1)} %fusion.179), channel_id=1, replica_groups=mesh['dp'=4,'mp'=8] {'mp'}, use_global_device_ids=true, to_apply=%region_26.27 | all-reduce | flops 512 | bytes 4096 | tf_op jit(solution)/shard_map/psum | solution.py:21
  879.6 12.4 add_add_fusion
  892.8 8.4 fusion.2
  905.2 80.2 %reduce-scatter.27.cloned.1.call-done = f32[2,24,24,128]{3,2,1,0:T(8,128)} async-done(((f32[2,24,24,1024]{3,2,1,0:T(8,128)}), f32[2,24,24,128]{3,2,1,0:T(8,128)}) %reduce-scatter.27.cloned.1.call-update) | async-done | bytes 589840 | tf_op jit(solution)/shard_map/reduce_scatter | solution.py:17
  987.7 39.6 %all-reduce.5 = (f32[2,24,24]{2,1,0:T(8,128)}, f32[2,24,24,1]{2,1,0,3:T(8,128)}) all-reduce(f32[2,24,24]{2,1,0:T(8,128)S(1)} %get-tuple-element.46, f32[2,24,24,1]{2,1,0,3:T(8,128)S(1)} %bitcast.520), channel_id=1, replica_groups=mesh['dp'=4,'mp'=8] {'mp'}, use_global_device_ids=true, to_apply=%region_31.32 | all-reduce | flops 2304 | bytes 18432 | tf_op jit(solution)/shard_map/psum | solution.py:21
  1042.5 9.4 convolution_bitcast_fusion
  1088.5 19.1 %reduce-scatter.15.cloned.1.call-done = f32[2,12,12,512]{3,2,1,0:T(8,128)} async-done(((f32[2,12,12,4096]{3,2,1,0:T(8,128)}), f32[2,12,12,512]{3,2,1,0:T(8,128)}) %reduce-scatter.15.cloned.1.call-update) | async-done | bytes 589840 | tf_op jit(solution)/shard_map/reduce_scatter | solution.py:17
  1109.9 31.2 %all-reduce.12.cloned.1.call-done = f32[2,128,256]{1,0,2:T(2,128)} async-done(((f32[2,128,256]{1,0,2:T(2,128)}), f32[2,128,256]{1,0,2:T(2,128)}) %all-reduce.12.cloned.1.call-update) | async-done | bytes 262160
  1149.2 91.6 %reduce-scatter.29.cloned.1.call-done = f32[2,24,24,128]{3,2,1,0:T(8,128)} async-done(((f32[2,24,24,1024]{3,2,1,0:T(8,128)}), f32[2,24,24,128]{3,2,1,0:T(8,128)}) %reduce-scatter.29.cloned.1.call-update) | async-done | bytes 589840 | tf_op jit(solution)/shard_map/reduce_scatter | solution.py:17
  1242.7 32.6 %reduce-scatter.39.cloned.1.call-done = f32[256,512]{1,0:T(8,128)} async-done(((f32[1024,512]{1,0:T(8,128)}), f32[256,512]{1,0:T(8,128)}) %reduce-scatter.39.cloned.1.call-update) | async-done | bytes 524304 | tf_op jit(solution)/shard_map/reduce_scatter | solution.py:267
  1275.3 27.9 %reduce-scatter.37.cloned.1.call-done = f32[2,128,256]{2,1,0:T(8,128)} async-done(((f32[2,128,1024]{2,1,0:T(8,128)}), f32[2,128,256]{2,1,0:T(8,128)}) %reduce-scatter.37.cloned.1.call-update) | async-done | bytes 262160 | tf_op jit(solution)/shard_map/reduce_scatter | solution.py:266
  1303.1 74.9 %reduce-scatter.41.cloned.1.call-done = f32[512,1024]{1,0:T(8,128)} async-done(((f32[512,4096]{1,0:T(8,128)}), f32[512,1024]{1,0:T(8,128)}) %reduce-scatter.41.cloned.1.call-update) | async-done | bytes 2097168 | tf_op jit(solution)/shard_map/reduce_scatter | solution.py:268
  1378.1 23.0 %reduce-scatter.35.cloned.1.call-done = f32[2,64,128]{2,1,0:T(8,128)} async-done(((f32[2,256,128]{2,1,0:T(8,128)}), f32[2,64,128]{2,1,0:T(8,128)}) %reduce-scatter.35.cloned.1.call-update) | async-done | bytes 65552 | tf_op jit(solution)/shard_map/reduce_scatter | solution.py:265
  1401.0 28.0 %reduce-scatter.31.cloned.1.call-done = f32[2,128,256]{2,1,0:T(8,128)} async-done(((f32[2,128,1024]{2,1,0:T(8,128)}), f32[2,128,256]{2,1,0:T(8,128)}) %reduce-scatter.31.cloned.1.call-update) | async-done | bytes 262160 | tf_op jit(solution)/shard_map/reduce_scatter | solution.py:262
  1429.0 81.5 %reduce-scatter.33.cloned.1.call-done = f32[2,128,9,256]{3,1,2,0:T(8,128)} async-done(((f32[2,128,9,1024]{3,1,2,0:T(8,128)}), f32[2,128,9,256]{3,1,2,0:T(8,128)}) %reduce-scatter.33.cloned.1.call-update) | async-done | bytes 2359312 | tf_op jit(solution)/shard_map/reduce_scatter | solution.py:263
  (347 shorter events, 182.7 us)
Async XLA Ops:
  7.2 377.1 %copy-start = (bf16[1024,512]{1,0:T(8,128)(2,1)S(1)}, bf16[1024,512]{1,0:T(8,128)(2,1)}, u32[]{:S(2)}) copy-start(bf16[1024,512]{1,0:T(8,128)(2,1)} %param.26) | copy-start | bytes 3145732
  7.2 94.9 %all-gather.4.cloned.1.call-start = ((), (), s32[]{:S(2)}) async-start(), calls=%async_computation.14 | async-start | bytes 2654208 | tf_op jit(solution)/shard_map/all_gather | solution.py:13
  51.0 137.3 %all-gather.6.cloned.1.call-start = ((), (), s32[]{:S(2)}) async-start(), calls=%async_computation.15 | async-start | bytes 2654208 | tf_op jit(solution)/shard_map/all_gather | solution.py:13
  137.1 249.5 %all-gather.8.cloned.1.call-start = ((), (), s32[]{:S(2)}) async-start(), calls=%async_computation.17 | async-start | bytes 3538944 | tf_op jit(solution)/shard_map/all_gather | solution.py:13
  140.2 319.2 %reduce-scatter.17.cloned.1.call-start = ((), (), s32[]{:S(2)}) async-start(), calls=%async_computation.18 | async-start | bytes 1769472 | tf_op jit(solution)/shard_map/reduce_scatter | solution.py:17
  396.6 131.7 %copy-start.25 = (f32[2,12,12,128]{3,2,1,0:T(8,128)S(1)}, f32[2,12,12,128]{3,2,1,0:T(8,128)}, u32[]{:S(2)}) copy-start(f32[2,12,12,128]{3,2,1,0:T(8,128)} %get-tuple-element.100) | copy-start | bytes 442372
  396.6 132.7 %copy-start.40 = (bf16[2,256,128]{2,1,0:T(8,128)(2,1)S(1)}, bf16[2,256,128]{2,1,0:T(8,128)(2,1)}, u32[]{:S(2)}) copy-start(bf16[2,256,128]{2,1,0:T(8,128)(2,1)} %param.23) | copy-start | bytes 393220
  396.6 132.6 %copy-start.43 = (f32[2,128]{1,0:T(2,128)S(1)}, f32[2,128]{1,0:T(2,128)}, u32[]{:S(2)}) copy-start(f32[2,128]{1,0:T(2,128)} %copy-done.42) | copy-start | bytes 3076
  396.7 164.7 %copy-start.51 = (f32[2,256]{1,0:T(2,128)S(1)}, f32[2,256]{1,0:T(2,128)}, u32[]{:S(2)}) copy-start(f32[2,256]{1,0:T(2,128)} %psum.131) | copy-start | bytes 6148
  396.7 164.7 %copy-start.60 = (f32[1,256]{1,0:T(1,128)S(1)}, f32[1,256]{1,0:T(1,128)}, u32[]{:S(2)}) copy-start(f32[1,256]{1,0:T(1,128)} %get-tuple-element.87) | copy-start | bytes 3076
  396.7 131.6 %reduce-scatter.19.cloned.1.call-start = ((), (), s32[]{:S(2)}) async-start(), calls=%async_computation.19 | async-start | bytes 1769472 | tf_op jit(solution)/shard_map/reduce_scatter | solution.py:17
  462.0 169.9 %reduce-scatter.21.cloned.1.call-start = ((), (), s32[]{:S(2)}) async-start(), calls=%async_computation.20 | async-start | bytes 1769472 | tf_op jit(solution)/shard_map/reduce_scatter | solution.py:17
  568.9 166.8 %copy-start.26 = (f32[2,12,12,128]{3,2,1,0:T(8,128)S(1)}, f32[2,12,12,128]{3,2,1,0:T(8,128)}, u32[]{:S(2)}) copy-start(f32[2,12,12,128]{3,2,1,0:T(8,128)} %reduce-scatter.17.cloned.1.call-done) | copy-start | bytes 442372
  568.9 166.8 %reduce-scatter.23.cloned.1.call-start = ((), (), s32[]{:S(2)}) async-start(), calls=%async_computation.21 | async-start | bytes 1769472 | tf_op jit(solution)/shard_map/reduce_scatter | solution.py:17
  672.6 162.6 %reduce-scatter.25.cloned.1.call-start = ((), (), s32[]{:S(2)}) async-start(), calls=%async_computation.22 | async-start | bytes 5308416 | tf_op jit(solution)/shard_map/reduce_scatter | solution.py:17
  740.5 96.0 %copy-start.41 = (bf16[2,256,128]{2,1,0:T(8,128)(2,1)S(1)}, bf16[2,256,128]{2,1,0:T(8,128)(2,1)}, u32[]{:S(2)}) copy-start(bf16[2,256,128]{2,1,0:T(8,128)(2,1)} %param.23) | copy-start | bytes 393220
  740.5 96.0 %copy-start.46 = (f32[2,128]{1,0:T(2,128)S(1)}, f32[2,128]{1,0:T(2,128)}, u32[]{:S(2)}) copy-start(f32[2,128]{1,0:T(2,128)} %copy-done.45) | copy-start | bytes 3076
  740.5 116.7 %copy-start.49 = (f32[2,256]{1,0:T(2,128)S(1)}, f32[2,256]{1,0:T(2,128)}, u32[]{:S(2)}) copy-start(f32[2,256]{1,0:T(2,128)} %copy-done.48) | copy-start | bytes 6148
  740.5 116.7 %copy-start.58 = (f32[1,256]{1,0:T(1,128)S(1)}, f32[1,256]{1,0:T(1,128)}, u32[]{:S(2)}) copy-start(f32[1,256]{1,0:T(1,128)} %copy-done.57) | copy-start | bytes 3076
  740.5 117.4 %copy-start.31 = (bf16[2,128,256]{2,1,0:T(8,128)(2,1)S(1)}, bf16[2,128,256]{2,1,0:T(8,128)(2,1)}, u32[]{:S(2)}) copy-start(bf16[2,128,256]{2,1,0:T(8,128)(2,1)} %param.21) | copy-start | bytes 393220
  740.5 244.8 %reduce-scatter.27.cloned.1.call-start = ((), (), s32[]{:S(2)}) async-start(), calls=%async_computation.23 | async-start | bytes 5308416 | tf_op jit(solution)/shard_map/reduce_scatter | solution.py:17
  892.1 215.5 %reduce-scatter.15.cloned.1.call-start = ((), (), s32[]{:S(2)}) async-start(), calls=%async_computation.16 | async-start | bytes 7077888 | tf_op jit(solution)/shard_map/reduce_scatter | solution.py:17
  901.3 239.8 %all-reduce.12.cloned.1.call-start = ((), (), s32[]{:S(2)}) async-start(), calls=%async_computation.31 | async-start | bytes 524288
  905.1 335.6 %reduce-scatter.29.cloned.1.call-start = ((), (), s32[]{:S(2)}) async-start(), calls=%async_computation.24 | async-start | bytes 5308416 | tf_op jit(solution)/shard_map/reduce_scatter | solution.py:17
  1034.5 240.8 %reduce-scatter.39.cloned.1.call-start = ((), (), s32[]{:S(2)}) async-start(), calls=%async_computation.29 | async-start | bytes 2621440 | tf_op jit(solution)/shard_map/reduce_scatter | solution.py:267
  1038.7 264.5 %reduce-scatter.37.cloned.1.call-start = ((), (), s32[]{:S(2)}) async-start(), calls=%async_computation.28 | async-start | bytes 1310720 | tf_op jit(solution)/shard_map/reduce_scatter | solution.py:266
  1042.4 335.6 %reduce-scatter.41.cloned.1.call-start = ((), (), s32[]{:S(2)}) async-start(), calls=%async_computation.30 | async-start | bytes 10485760 | tf_op jit(solution)/shard_map/reduce_scatter | solution.py:268
  1051.9 349.1 %reduce-scatter.35.cloned.1.call-start = ((), (), s32[]{:S(2)}) async-start(), calls=%async_computation.27 | async-start | bytes 327680 | tf_op jit(solution)/shard_map/reduce_scatter | solution.py:265
  1062.2 366.8 %reduce-scatter.31.cloned.1.call-start = ((), (), s32[]{:S(2)}) async-start(), calls=%async_computation.25 | async-start | bytes 1310720 | tf_op jit(solution)/shard_map/reduce_scatter | solution.py:262
  1067.9 442.6 %reduce-scatter.33.cloned.1.call-start = ((), (), s32[]{:S(2)}) async-start(), calls=%async_computation.26 | async-start | bytes 11796480 | tf_op jit(solution)/shard_map/reduce_scatter | solution.py:263
  1086.7 154.0 %copy-start.18 = (f32[2,24,12,2,128]{4,3,2,1,0:T(2,128)S(1)}, f32[2,24,12,2,128]{4,3,2,1,0:T(2,128)}, u32[]{:S(2)}) copy-start(f32[2,24,12,2,128]{4,3,2,1,0:T(2,128)} %copy-done.17) | copy-start | bytes 1769476
  1086.8 423.8 %copy-start.1 = (bf16[1024,512]{1,0:T(8,128)(2,1)S(1)}, bf16[1024,512]{1,0:T(8,128)(2,1)}, u32[]{:S(2)}) copy-start(bf16[1024,512]{1,0:T(8,128)(2,1)} %param.26) | copy-start | bytes 3145732
  (75 other events, 1620.6 us)
Sparse Core Ops, SparseCore 0:
  51.1 51.0 all-gather.3
  137.2 51.0 all-gather.5
  190.9 72.6 all-gather.7
  396.7 62.6 reduce-scatter.16
  463.7 64.4 reduce-scatter.18
  569.0 62.9 reduce-scatter.20
  672.8 62.9 reduce-scatter.22
  740.6 94.5 reduce-scatter.24
  892.2 93.0 reduce-scatter.26
  988.8 118.7 reduce-scatter.14
  1109.9 31.1 all-reduce.11
  1145.1 95.6 reduce-scatter.28
  1244.0 31.1 reduce-scatter.38
  1278.2 24.8 reduce-scatter.36
  1306.3 71.6 reduce-scatter.40
  1380.9 20.0 reduce-scatter.34
  1404.1 24.8 reduce-scatter.30
  1432.1 78.4 reduce-scatter.32
where the time goes:
time: 1530 us; the launch traced here: 1520 us
  waiting for transfers between devices  932 us (61%)
  blocking collectives  363 us (24%)
  matrix products  138 us (9%)
  other arithmetic  42.1 us (3%)
  local copies, waits for them, and re-layouts  24.4 us (2%)
  between operations  16.5 us (1%)
    reduce_scatter x8, waiting for transfers between devices, channel_share(): return lax.psum_scatter(value, 'mp', scatter_dimension=3, tiled=True)  540 us
    psum x8, blocking collectives, channel_total(): return lax.psum(value, 'mp')  238 us
    all_gather x4, blocking collectives, all_channels(): return lax.all_gather(value, 'mp', axis=3, tiled=True)  118 us
    all_gather x3, waiting for transfers between devices, all_channels(): return lax.all_gather(value, 'mp', axis=3, tiled=True)  92.5 us
    reduce_scatter x1, waiting for transfers between devices, on_device(): lax.psum_scatter(stacked[3], 'dp', scatter_dimension=3, tiled=True)  81.5 us
    reduce_scatter x1, waiting for transfers between devices, on_device(): lax.psum_scatter(grad_w_read2, 'dp', scatter_dimension=1, tiled=True)  74.9 us
    dot_general x24, matrix products, project(): jnp.einsum('bijc,cd->bijd', left, weight, preferred_element_type=jnp.floa...  60.8 us
    dot_general x24, matrix products, project_t(): jnp.einsum('bijc,dc->bijd', left, weight, preferred_element_type=jnp.floa...  36.4 us
  transfers between devices with their start and end apart: 18, of which 17 were waited for; matrix products, arithmetic and copies ran while one was open for 7% of the time, Pallas kernels for 0%

commit v1 on v0

v1 whole, which is shorter than its diff:
```python
from functools import partial

import jax
import jax.numpy as jnp
from jax import lax
from jax.experimental import pallas as pl
from jax.experimental.pallas import tpu as pltpu
from jax.sharding import PartitionSpec as P

epsilon = 1e-06
highest = lax.Precision.HIGHEST
f32 = jnp.float32
bf16 = jnp.bfloat16
MESH = pl.DeviceIdType.MESH
VMEM_LIMIT = 56 << 20


def vmem_specs(count):
    return [pl.BlockSpec(memory_space=pltpu.VMEM)] * count


def barrier(peers):
    sem = pltpu.get_barrier_semaphore()
    for peer in peers:
        pl.semaphore_signal(sem, inc=1, device_id=peer, device_id_type=MESH)
    pl.semaphore_wait(sem, len(peers))


def sent(src, dst, send_sem, recv_sem, peer):
    return pltpu.make_async_remote_copy(
        src_ref=src,
        dst_ref=dst,
        send_sem=send_sem,
        recv_sem=recv_sem,
        device_id=peer,
        device_id_type=MESH,
    )


def exchange_kernel(size, kinds, *refs):
    count = len(kinds)
    sources, results = refs[:count], refs[count : 2 * count]
    slots = list(refs[2 * count : -2])
    send_sem, recv_sem = refs[-2:]
    landing = [slots.pop(0) if kind in ("rs", "psum") else result for kind, result in zip(kinds, results)]
    dp, mp = lax.axis_index("dp"), lax.axis_index("mp")
    peers = [(dp, lax.rem(mp + step, size)) for step in range(1, size)]
    barrier(peers)
    copies = []
    for index, kind in enumerate(kinds):
        for step, peer in enumerate(peers):
            src = sources[index].at[peer[1]] if kind in ("rs", "a2a") else sources[index]
            copy = sent(
                src, landing[index].at[mp], send_sem.at[index, step], recv_sem.at[index, step], peer
            )
            copy.start()
            copies.append(copy)
    for index, kind in enumerate(kinds):
        if kind in ("rs", "a2a"):
            landing[index][mp] = sources[index][mp]
        else:
            landing[index][mp] = sources[index][...]
    for copy in copies:
        copy.wait()
    for index, kind in enumerate(kinds):
        if kind in ("rs", "psum"):
            total = landing[index][0].astype(f32)
            for step in range(1, size):
                total = total + landing[index][step].astype(f32)
            results[index][...] = total


def exchange(name, collective, size, *pairs):
    kinds = tuple(kind for kind, value in pairs)
    values = [value for kind, value in pairs]
    shapes, scratch = [], []
    for kind, value in pairs:
        block = value.shape[1:] if kind in ("rs", "a2a") else value.shape
        if kind in ("rs", "psum"):
            shapes.append(jax.ShapeDtypeStruct(block, f32))
            scratch.append(pltpu.VMEM((size,) + block, value.dtype))
        else:
            shapes.append(jax.ShapeDtypeStruct((size,) + block, value.dtype))
    sems = pltpu.SemaphoreType.DMA((len(pairs), size - 1))
    return pl.pallas_call(
        partial(exchange_kernel, size, kinds),
        name=name,
        out_shape=shapes,
        in_specs=vmem_specs(len(values)),
        out_specs=vmem_specs(len(values)),
        scratch_shapes=scratch + [sems, sems],
        compiler_params=pltpu.CompilerParams(
            collective_id=collective, has_side_effects=True, vmem_limit_bytes=VMEM_LIMIT
        ),
    )(*values)


def weights_kernel(size, w_ref, gb_ref, out_ref, gb_out, ss, rs, cs, cr, gs, gr):
    dp, mp = lax.axis_index("dp"), lax.axis_index("mp")
    core = lax.rem(dp, 2)
    sibling = (dp + 1 - 2 * core, mp)
    peers = [(dp, lax.rem(mp + step, size)) for step in range(1, size)]
    barrier(peers + [sibling])
    count, rows = w_ref.shape[0], w_ref.shape[1]
    half = rows // 2
    mine = pl.ds(pl.multiple_of(core * half, half), half)

    def part(owner):
        return pl.ds(pl.multiple_of(owner * rows + core * half, half), half)

    copies = []
    for step, peer in enumerate(peers):
        copy = sent(gb_ref, gb_out.at[mp], gs.at[step], gr.at[step], peer)
        copy.start()
        copies.append(copy)
    outgoing = {}
    for which in range(count):
        for step, peer in enumerate(peers):
            copy = sent(
                w_ref.at[which, mine],
                out_ref.at[which, part(mp)],
                ss.at[which, step],
                rs.at[which, step],
                peer,
            )
            copy.start()
            outgoing[which, step] = copy
    gb_out[mp] = gb_ref[...]
    for which in range(count):
        out_ref[which, pl.ds(pl.multiple_of(mp * rows, rows), rows), :] = w_ref[which]
    for which in range(count):
        for step in range(size - 1):
            owner = lax.rem(mp + size - 1 - step, size)
            outgoing[which, step].wait_recv()
            copy = sent(
                out_ref.at[which, part(owner)],
                out_ref.at[which, part(owner)],
                cs.at[which, step],
                cr.at[which, step],
                sibling,
            )
            copy.start()
            copies.append(copy)
    for copy in outgoing.values():
        copy.wait_send()
    for copy in copies:
        copy.wait()


def gather_weights(size, weights, vectors):
    count, rows, width = weights.shape
    sem = pltpu.SemaphoreType.DMA((count, size - 1))
    vector_sem = pltpu.SemaphoreType.DMA((size - 1,))
    return pl.pallas_call(
        partial(weights_kernel, size),
        name="gather_weights",
        out_shape=[
            jax.ShapeDtypeStruct((count, rows * size, width), weights.dtype),
            jax.ShapeDtypeStruct((size,) + vectors.shape, vectors.dtype),
        ],
        in_specs=vmem_specs(2),
        out_specs=vmem_specs(2),
        scratch_shapes=[sem, sem, sem, sem, vector_sem, vector_sem],
        compiler_params=pltpu.CompilerParams(
            collective_id=1, has_side_effects=True, vmem_limit_bytes=VMEM_LIMIT
        ),
    )(weights, vectors)


def dp_kernel(size, *refs):
    count = (len(refs) - 4) // 4
    sources = refs[:count]
    results = refs[count : 2 * count]
    first = refs[2 * count : 3 * count]
    second = refs[3 * count : 4 * count]
    cs, cr, ys, yr = refs[4 * count :]
    dp, mp = lax.axis_index("dp"), lax.axis_index("mp")
    core = lax.rem(dp, 2)
    y = lax.div(dp, 2)
    chips = size // 2
    sibling = (dp + 1 - 2 * core, mp)
    others = [(2 * lax.rem(y + step, chips) + core, mp) for step in range(1, chips)]
    barrier([sibling] + others)
    copies = []
    for index in range(count):
        for chip in range(chips):
            copy = sent(
                sources[index].at[2 * chip + 1 - core],
                first[index].at[chip],
                cs.at[index, chip],
                cr.at[index, chip],
                sibling,
            )
            copy.start()
            copies.append(copy)
    late = []
    for index in range(count):
        for chip in range(chips):
            copies[index * chips + chip].wait_recv()
            first[index][chip] = (
                first[index][chip].astype(f32) + sources[index][2 * chip + core].astype(f32)
            ).astype(first[index].dtype)
        for step, peer in enumerate(others):
            copy = sent(
                first[index].at[lax.rem(y + step + 1, chips)],
                second[index].at[step],
                ys.at[index, step],
                yr.at[index, step],
                peer,
            )
            copy.start()
            late.append((index, copy))
    for index in range(count):
        total = first[index][y].astype(f32)
        for step in range(chips - 1):
            late[index * (chips - 1) + step][1].wait_recv()
            total = total + second[index][step].astype(f32)
        results[index][...] = total
    for copy in copies:
        copy.wait_send()
    for index, copy in late:
        copy.wait_send()


def dp_scatter(size, values):
    count, chips = len(values), size // 2
    first = [pltpu.VMEM((chips,) + value.shape[1:], value.dtype) for value in values]
    second = [pltpu.VMEM((max(chips - 1, 1),) + value.shape[1:], value.dtype) for value in values]
    core_sem = pltpu.SemaphoreType.DMA((count, chips))
    y_sem = pltpu.SemaphoreType.DMA((count, max(chips - 1, 1)))
    return pl.pallas_call(
        partial(dp_kernel, size),
        name="dp_scatter",
        out_shape=[jax.ShapeDtypeStruct(value.shape[1:], f32) for value in values],
        in_specs=vmem_specs(count),
        out_specs=vmem_specs(count),
        scratch_shapes=first + second + [core_sem, core_sem, y_sem, y_sem],
        compiler_params=pltpu.CompilerParams(
            collective_id=2, has_side_effects=True, vmem_limit_bytes=VMEM_LIMIT
        ),
    )(*values)


def nt(left, right):
    return lax.dot_general(left, right, (((1,), (1,)), ((), ())), preferred_element_type=f32)


def nn(left, right):
    return lax.dot_general(left, right, (((1,), (0,)), ((), ())), preferred_element_type=f32)


def tn(left, right):
    return lax.dot_general(left, right, (((0,), (0,)), ((), ())), preferred_element_type=f32)


def exact(left, right):
    return jnp.dot(left, right, precision=highest)


def blocks_to_wide(value):
    return jnp.swapaxes(value, 0, 1).reshape(value.shape[1], -1)


def wide_to_blocks(value, count):
    return jnp.swapaxes(value.reshape(value.shape[0], count, -1), 0, 1)


def normalize(h):
    mean = jnp.mean(h, axis=1, keepdims=True)
    centered = h - mean
    inv_std = lax.rsqrt(jnp.mean(centered * centered, axis=1, keepdims=True) + epsilon)
    return centered * inv_std, inv_std


def conv_forward(norm, w_conv, images, side):
    width = norm.shape[1]
    out = lax.conv_general_dilated(
        norm.reshape(images, side, side, width),
        w_conv.reshape(w_conv.shape[0], 3, 3, width),
        (1, 1),
        ((1, 1), (1, 1)),
        dimension_numbers=("NHWC", "OHWI", "NHWC"),
        preferred_element_type=f32,
    )
    return out.reshape(images, side * side, -1)


def shifted(grad_conv, images, side):
    width = grad_conv.shape[1]
    padded = jnp.pad(grad_conv.reshape(images, side, side, width), ((0, 0), (1, 1), (1, 1), (0, 0)))
    parts = [
        padded[:, 2 - tap // 3 : 2 - tap // 3 + side, 2 - tap % 3 : 2 - tap % 3 + side, :]
        for tap in range(9)
    ]
    return jnp.stack(parts, axis=3).reshape(images * side * side, 9 * width)


def pool(value, images, side):
    half = side // 2
    shape = (images, half, 2, half, 2, value.shape[-1])
    return jnp.mean(value.astype(f32).reshape(shape), axis=(2, 4)).reshape(images * half * half, -1)


def spread(value, images, half):
    grid = value.reshape(images, half, 1, half, 1, value.shape[-1])
    full = jnp.broadcast_to(grid, (images, half, 2, half, 2, value.shape[-1]))
    return full.reshape(images * 4 * half * half, -1)


def gelu_parts(value):
    cdf = 0.5 * (1.0 + lax.erf(value * (0.5**0.5)))
    pdf = jnp.exp(-0.5 * value * value) * ((2.0 * jnp.pi) ** -0.5)
    return value * cdf, cdf + value * pdf


def silu_grad(value):
    gate = jax.nn.sigmoid(value)
    return gate * (1.0 + value * (1.0 - gate))


def row_share(value, start, rows):
    return lax.dynamic_slice_in_dim(value, start, rows, 0)


def on_device(
    mp_size,
    dp_size,
    features,
    w_in,
    ln_gain,
    ln_bias,
    w_conv,
    se_down,
    se_down_bias,
    se_up,
    se_up_bias,
    w_out,
    w_read1,
    b_read1,
    w_read2,
    b_read2,
    out_grad,
    box_counts,
):
    images, side, _, width = features.shape
    half = side // 2
    local = w_in.shape[1]
    rows = (images * side * side, images * half * half)
    sides = (side, half)
    share = (rows[0] // mp_size, rows[1] // mp_size)
    mp = lax.axis_index("mp")

    def ex(name, collective, *pairs):
        return exchange(name, collective, mp_size, *pairs)

    feats = features.reshape(rows[0], width)
    grad_top = (
        out_grad.astype(f32) * box_counts.astype(f32)[:, None, None, None]
    ).astype(bf16).reshape(rows[1], -1)
    grad_b_read2 = jnp.sum(grad_top.astype(f32), axis=0)
    weights, vectors = gather_weights(
        mp_size,
        jnp.stack([w_in[0], w_out[0], w_in[1], w_out[1]]),
        jnp.concatenate([ln_gain, ln_bias], axis=0),
    )
    (grad_full,) = ex("gather_dout", 3, ("ag", grad_top))
    wide_in = (weights[0], weights[2])
    wide_out = (weights[1], weights[3])
    vectors = jnp.swapaxes(vectors, 0, 1).reshape(4, width)
    gains, shifts = vectors[:2], vectors[2:]

    def forward(index, low):
        h = nt(low, wide_in[index])
        normed, inv_std = normalize(h)
        norm = (normed * gains[index] + shifts[index]).astype(bf16)
        conv = conv_forward(norm, w_conv[index], images, sides[index])
        act = jax.nn.silu(conv)
        pooled = jnp.mean(act, axis=1)
        (pre_down,) = ex(
            "squeeze", 4 + index, ("psum", exact(pooled, se_down[index].astype(f32)))
        )
        pre_down = pre_down + se_down_bias[index]
        squeeze = jax.nn.silu(pre_down)
        excite = jax.nn.sigmoid(exact(squeeze, se_up[index].astype(f32)) + se_up_bias[index])
        scaled = act * excite[:, None, :]
        own_h = row_share(h, mp * share[index], share[index])
        return norm, conv, act, pooled, pre_down, squeeze, excite, scaled, own_h

    first = forward(0, feats)
    mean_scaled = pool(first[7].reshape(rows[0], -1), images, side).astype(bf16)
    (mean_scaled,) = ex("gather_scaled0", 6, ("ag", mean_scaled))
    mean_scaled = blocks_to_wide(mean_scaled)
    value = pool(feats, images, side) + nt(mean_scaled, wide_out[0])
    value_low = value.astype(bf16)
    second = forward(1, value_low)
    (scaled1,) = ex("gather_scaled1", 7, ("ag", second[7].reshape(rows[1], -1).astype(bf16)))
    scaled1 = blocks_to_wide(scaled1)
    top = (value + nt(scaled1, wide_out[1])).astype(bf16)
    act_full, slope = gelu_parts(nn(top, w_read1) + b_read1)
    act_low = act_full.astype(bf16)
    grad_full = blocks_to_wide(grad_full)
    grad_pre = (nt(grad_full, w_read2) * slope).astype(bf16)
    grad_b_read1 = jnp.sum(grad_pre.astype(f32), axis=0)
    (grad_out,) = ex(
        "scatter_g", 8, ("rs", nt(grad_pre, w_read1).astype(bf16).reshape(mp_size, share[1], width))
    )
    (readout,) = ex(
        "scatter_readout", 9, ("rs", wide_to_blocks(nn(act_low, w_read2).astype(bf16), mp_size))
    )
    readout = (readout + b_read2).astype(bf16).reshape(images, half, half, -1)
    grad_w_read2 = tn(act_low, grad_full)
    grad_w_read1 = tn(top, grad_pre)

    def to_channels(name, collective, *values):
        stacked = jnp.concatenate([wide_to_blocks(value, mp_size) for value in values], axis=1)
        (result,) = ex(name, collective, ("a2a", stacked))
        parts, start = [], 0
        for value in values:
            part = result[:, start : start + value.shape[0]]
            start += value.shape[0]
            parts.append(part)
        return parts

    def backward(index, grad_scaled, saved):
        norm, conv, act, pooled, pre_down, squeeze, excite, scaled, own_h = saved
        here = sides[index]
        gate_grad = jnp.sum(grad_scaled * act, axis=1)
        grad_up = gate_grad * excite * (1.0 - excite)
        (grad_squeeze,) = ex(
            "squeeze_back", 10 + index, ("psum", exact(grad_up, se_up[index].astype(f32).T))
        )
        grad_down = grad_squeeze * silu_grad(pre_down)
        grad_pooled = exact(grad_down, se_down[index].astype(f32).T)
        grad_act = grad_scaled * excite[:, None, :] + grad_pooled[:, None, :] / (here * here)
        grad_conv = (grad_act * silu_grad(conv)).astype(bf16).reshape(rows[index], -1)
        taps = shifted(grad_conv, images, here)
        grad_w_conv = tn(taps, norm).reshape(9, local, width)
        taps_weight = jnp.swapaxes(w_conv[index], 0, 1).reshape(9 * local, width)
        partial_norm = nn(taps, taps_weight).astype(bf16)
        (grad_norm,) = ex(
            "scatter_norm", 12 + index, ("rs", partial_norm.reshape(mp_size, share[index], width))
        )
        normed, inv_std = normalize(own_h)
        grad_gain = jnp.sum(grad_norm * normed, axis=0)
        grad_shift = jnp.sum(grad_norm, axis=0)
        scaled_grad = grad_norm * gains[index]
        grad_h = (
            inv_std
            * (
                scaled_grad
                - jnp.mean(scaled_grad, axis=1, keepdims=True)
                - normed * jnp.mean(scaled_grad * normed, axis=1, keepdims=True)
            )
        ).astype(bf16)
        small = (
            exact(squeeze.T, grad_up),
            jnp.sum(grad_up, axis=0),
            exact(pooled.T, grad_down),
            jnp.sum(grad_down, axis=0),
        )
        return grad_w_conv, grad_h, jnp.stack([grad_gain, grad_shift]), small

    grad_low = grad_out.astype(bf16)
    gs1, gy1 = to_channels("spread1", 14, nn(grad_low, wide_out[1]).astype(bf16), grad_low)
    gs1 = gs1.astype(f32).reshape(images, half * half, local)
    grad_w_out1 = tn(gy1.reshape(rows[1], local), scaled1)
    grad_w_conv1, grad_h1, lines1, small1 = backward(1, gs1, second)
    grad_value = (grad_out + nn(grad_h1, wide_in[1])) * 0.25
    grad_value_low = grad_value.astype(bf16)
    gs0, gy0, gh1 = to_channels(
        "spread0", 15, nn(grad_value_low, wide_out[0]).astype(bf16), grad_value_low, grad_h1
    )
    grad_w_in1 = tn(gh1.reshape(rows[1], local), value_low)
    grad_w_out0 = 4.0 * tn(gy0.reshape(rows[1], local), mean_scaled)
    residual = spread(gy0.astype(f32).reshape(rows[1], local), images, half)
    gs0 = spread(gs0.astype(f32).reshape(rows[1], local), images, half)
    grad_w_conv0, grad_h0, lines0, small0 = backward(
        0, gs0.reshape(images, side * side, local), first
    )
    grad_in = nn(grad_h0, wide_in[0]).astype(bf16)
    lines = jnp.concatenate([lines0, lines1], axis=0)
    stacked = jnp.concatenate(
        [wide_to_blocks(grad_in, mp_size), wide_to_blocks(grad_h0, mp_size)], axis=1
    )
    spread_all, lines = ex(
        "spread_last", 16, ("a2a", stacked), ("rs", wide_to_blocks(lines, mp_size))
    )
    grad_features = spread_all[:, : share[0]].astype(f32).reshape(rows[0], local) + residual
    grad_features = grad_features.reshape(images, side, side, local)
    grad_w_in0 = tn(spread_all[:, share[0] :].reshape(rows[0], local), feats)

    def parted(value, axis):
        shape = value.shape
        split = value.reshape(shape[:axis] + (dp_size, shape[axis] // dp_size) + shape[axis + 1 :])
        return jnp.moveaxis(split, axis, 0)

    scattered = dp_scatter(
        dp_size,
        [
            parted(jnp.stack([grad_w_in0, grad_w_in1]).astype(bf16), 2),
            parted(jnp.stack([grad_w_conv0, grad_w_conv1]).astype(bf16), 3),
            parted(jnp.stack([small0[2], small1[2]]).astype(bf16), 2),
            parted(jnp.stack([small0[0], small1[0]]).astype(bf16), 1),
            parted(jnp.stack([grad_w_out0, grad_w_out1]).astype(bf16), 2),
            parted(grad_w_read1.astype(bf16), 0),
            parted(grad_w_read2.astype(bf16), 1),
        ],
    )
    vectors = lax.psum(
        (
            lines[0::2],
            lines[1::2],
            jnp.stack([small0[3], small1[3]]),
            jnp.stack([small0[1], small1[1]]),
            grad_b_read1,
            grad_b_read2,
        ),
        "dp",
    )
    return (
        readout,
        grad_features,
        scattered[0],
        vectors[0],
        vectors[1],
        jnp.swapaxes(scattered[1], 1, 2),
        scattered[2],
        vectors[2],
        scattered[3],
        vectors[3],
        scattered[4],
        scattered[5],
        vectors[4],
        scattered[6],
        vectors[5],
    )


def solution(mesh):
    in_specs = (
        P("dp", None, None, None),
        P(None, "mp", None),
        P(None, "mp"),
        P(None, "mp"),
        P(None, "mp", None, None),
        P(None, "mp", None),
        P(),
        P(None, None, "mp"),
        P(None, "mp"),
        P(None, "mp", None),
        P(None, "mp"),
        P("mp"),
        P("mp", None),
        P("mp"),
        P("dp", None, None, "mp"),
        P("dp"),
    )
    out_specs = (
        P("dp", None, None, "mp"),
        P("dp", None, None, "mp"),
        P(None, "mp", "dp"),
        P(None, "mp"),
        P(None, "mp"),
        P(None, "mp", None, "dp"),
        P(None, "mp", "dp"),
        P(),
        P(None, "dp", "mp"),
        P(None, "mp"),
        P(None, "mp", "dp"),
        P("dp", "mp"),
        P("mp"),
        P("mp", "dp"),
        P("mp"),
    )
    body = partial(on_device, mesh.shape["mp"], mesh.shape["dp"])
    return jax.shard_map(
        body, mesh=mesh, in_specs=in_specs, out_specs=out_specs, check_vma=False
    )
```

time: 1530 us -> 723 us (0.47)
  waiting for transfers between devices: 932 us -> 0 us
  Pallas kernels: 0 us -> 478 us
  blocking collectives: 363 us -> 6.57 us
  local copies, waits for them, and re-layouts: 24.4 us -> 93.8 us
  matrix products: 138 us -> 81.9 us
    reduce_scatter x14 -> x0, waiting for transfers between devices: 808 us -> none  [the longest x8 540 us: channel_share(): return lax.psum_scatter(value, 'mp', scatter_dimension=3, tiled=True)]
    pallas_call x0 -> x16, Pallas kernels: none -> 478 us  [the longest x14 307 us: exchange(): pl.pallas_call(partial(exchange_kernel, size, kinds), name=name, out_shap...]
    psum x9 -> x1, blocking collectives: 245 us -> 6.57 us  [on_device(): lax.psum((lines[0::2], lines[1::2], jnp.stack([small0[3], small1[3]]), jn...]
    all_gather x4 -> x0, blocking collectives: 118 us -> none  [all_channels(): return lax.all_gather(value, 'mp', axis=3, tiled=True)]
    all_gather x3 -> x0, waiting for transfers between devices: 92.5 us -> none  [all_channels(): return lax.all_gather(value, 'mp', axis=3, tiled=True)]
    dot_general x84 -> x34, matrix products: 138 us -> 60.5 us  [the longest x8 19.2 us: tn(): lax.dot_general(left, right, (((0,), (0,)), ((), ())), preferred_element_...]
    unnamed x19 -> x0, waiting for transfers between devices: 31.5 us -> none
    conv_general_dilated x0 -> x2, matrix products: none -> 21.4 us  [conv_forward(): lax.conv_general_dilated(norm.reshape(images, side, side, width), w_conv....]
  transfers between devices with their start and end apart: 18 -> 0, of which waited for: 17 -> 0; matrix products, arithmetic and copies ran while one was open for 7% -> 0% of each run, Pallas kernels for 0% -> 0%
where the time goes in v1:
time: 723 us; the launch traced here: 712 us
  Pallas kernels  478 us (66%)
  local copies, waits for them, and re-layouts  93.8 us (13%)
  matrix products  81.9 us (11%)
  other arithmetic  49.7 us (7%)
    pallas_call x14, Pallas kernels, exchange(): pl.pallas_call(partial(exchange_kernel, size, kinds), name=name, out_shap...  307 us
    pallas_call x1, Pallas kernels, gather_weights(): pl.pallas_call(partial(weights_kernel, size), name='gather_weights', out_...  96.6 us
    pallas_call x1, Pallas kernels, dp_scatter(): pl.pallas_call(partial(dp_kernel, size), name='dp_scatter', out_shape=[ja...  73.8 us
    unnamed x204, local copies, waits for them, and re-layouts  29.9 us
    conv_general_dilated x2, matrix products, conv_forward(): lax.conv_general_dilated(norm.reshape(images, side, side, width), w_conv....  21.4 us
    dot_general x8, matrix products, tn(): lax.dot_general(left, right, (((0,), (0,)), ((), ())), preferred_element_...  19.2 us
    dot_general x6, matrix products, nt(): lax.dot_general(left, right, (((1,), (1,)), ((), ())), preferred_element_...  17.1 us
    dot_general x8, matrix products, nn(): lax.dot_general(left, right, (((1,), (0,)), ((), ())), preferred_element_...  15.9 us

profile of v1, /device:TPU:0, one launch (start us, length us, event | category | flops | bytes accessed | tf_op | source)
XLA Modules:
  0.0 712.4 jit_solution(743086964568411391)
XLA Ops:
  0.7 6.3 reshape.402
  7.0 6.2 reduce_sum.259
  18.7 96.6 %gather_weights.1 = (bf16[4,1024,1024]{2,1,0:T(8,128)(2,1)}, f32[8,4,128]{2,1,0:T(4,128)}) custom-call(bf16[4,128,1024]{2,1,0:T(8,128)(2,1)} %pad_maximum_fusion.w_ref, f32[4,128]{1,0:T(4,128)} %pad_maximum_fusion.4.gb_ref), custom_call_target="tpu_custom_call" | custom-call | tf_op jit(solution)/shard_map/gather_weights/pallas_call | solution.py:154
  115.4 5.4 fusion.137
  120.9 4.5 fusion.145
  131.5 15.7 %fusion.135 = (f32[2,128]{1,0:T(2,128)S(1)}, f32[2,24,24,128]{3,0,2,1:T(2,128)}, f32[2,24,24,128]{3,0,2,1:T(2,128)S(1)}) fusion(bf16[128,3,3,1024]{3,0,2,1:T(8,128)(2,1)} %bitcast.385, bf16[2,24,24,1024]{3,2,1,0:T(8,128)(2,1)} %bitcast.379), kind=kOutput, calls=%fused_computation.242 | convolution fusion | flops 2569748224 | bytes 5899264 | tf_op jit(solution)/shard_map/conv_general_dilated | solution.py:277
  148.5 14.5 %squeeze.46 = f32[2,256]{1,0:T(2,128)} custom-call(f32[2,256]{1,0:T(2,128)} %fusion.107.refs_0_), custom_call_target="tpu_custom_call" | custom-call | tf_op jit(solution)/shard_map/squeeze/pallas_call | solution.py:85
  165.9 14.8 %gather_scaled0.1 = bf16[8,288,128]{2,1,0:T(8,128)(2,1)} custom-call(bf16[288,128]{1,0:T(8,128)(2,1)} %convert_element_type.138.refs_0_), custom_call_target="tpu_custom_call" | custom-call | tf_op jit(solution)/shard_map/gather_scaled0/pallas_call | solution.py:85
  180.7 3.6 fusion.146
  191.5 5.7 multiply_reduce_fusion.10
  201.1 11.1 %squeeze.47 = f32[2,256]{1,0:T(2,128)} custom-call(f32[2,256]{1,0:T(2,128)} %fusion.101.refs_0_), custom_call_target="tpu_custom_call" | custom-call | tf_op jit(solution)/shard_map/squeeze/pallas_call | solution.py:85
  215.3 13.8 %gather_scaled1.1 = bf16[8,288,128]{2,1,0:T(8,128)(2,1)} custom-call(bf16[288,128]{1,0:T(8,128)(2,1)} %fusion.93.refs_0_), custom_call_target="tpu_custom_call" | custom-call | tf_op jit(solution)/shard_map/gather_scaled1/pallas_call | solution.py:85
  236.6 44.9 %scatter_readout.1 = f32[288,512]{1,0:T(8,128)} custom-call(bf16[8,288,512]{2,1,0:T(8,128)(2,1)} %bitcast.366), custom_call_target="tpu_custom_call" | custom-call | tf_op jit(solution)/shard_map/scatter_readout/pallas_call | solution.py:85
  292.4 55.7 %gather_dout.1 = bf16[8,288,512]{2,1,0:T(8,128)(2,1)} custom-call(bf16[288,512]{1,0:T(8,128)(2,1)} %reshape.373.refs_0_), custom_call_target="tpu_custom_call" | custom-call | tf_op jit(solution)/shard_map/gather_dout/pallas_call | solution.py:85
  357.2 29.0 %scatter_g.1 = f32[36,1024]{1,0:T(8,128)} custom-call(bf16[8,36,1024]{2,1,0:T(8,128)(2,1)} %reshape.375.refs_0_), custom_call_target="tpu_custom_call" | custom-call | tf_op jit(solution)/shard_map/scatter_g/pallas_call | solution.py:85
  390.1 11.5 %spread1.1 = bf16[8,72,128]{2,1,0:T(8,128)(2,1)} custom-call(bf16[8,72,128]{2,1,0:T(8,128)(2,1)} %pad_maximum_fusion.3.refs_0_), custom_call_target="tpu_custom_call" | custom-call | tf_op jit(solution)/shard_map/spread1/pallas_call | solution.py:85
  405.1 7.9 %squeeze_back.2 = f32[2,256]{1,0:T(2,128)} custom-call(f32[2,256]{1,0:T(2,128)} %fusion.97.refs_0_), custom_call_target="tpu_custom_call" | custom-call | tf_op jit(solution)/shard_map/squeeze_back/pallas_call | solution.py:85
  419.3 13.5 %scatter_norm.2 = f32[36,1024]{1,0:T(8,128)} custom-call(bf16[8,36,1024]{2,1,0:T(8,128)(2,1)} %reshape.382.refs_0_), custom_call_target="tpu_custom_call" | custom-call | tf_op jit(solution)/shard_map/scatter_norm/pallas_call | solution.py:85
  440.4 12.1 %spread0.1 = bf16[8,108,128]{2,1,0:T(8,128)(2,1)} custom-call(bf16[8,108,128]{2,1,0:T(8,128)(2,1)} %pad_maximum_fusion.2.refs_0_), custom_call_target="tpu_custom_call" | custom-call | tf_op jit(solution)/shard_map/spread0/pallas_call | solution.py:85
  458.8 8.1 %squeeze_back.3 = f32[2,256]{1,0:T(2,128)} custom-call(f32[2,256]{1,0:T(2,128)} %fusion.103.refs_0_), custom_call_target="tpu_custom_call" | custom-call | tf_op jit(solution)/shard_map/squeeze_back/pallas_call | solution.py:85
  473.9 4.7 convolution_convert_fusion.2
  478.7 39.1 %scatter_norm.3 = f32[144,1024]{1,0:T(8,128)} custom-call(bf16[8,144,1024]{2,1,0:T(8,128)(2,1)} %bitcast.380), custom_call_target="tpu_custom_call" | custom-call | tf_op jit(solution)/shard_map/scatter_norm/pallas_call | solution.py:85
  526.7 31.7 %spread_last.1 = (bf16[8,288,128]{2,1,0:T(8,128)(2,1)}, f32[4,128]{1,0:T(4,128)}) custom-call(bf16[8,288,128]{2,1,0:T(8,128)(2,1)} %pad_maximum_fusion.1.refs_0_, f32[8,4,128]{2,1,0:T(4,128)} %maximum_bitcast_fusion.5.refs_1_), custom_call_target="tpu_custom_call" | custom-call | tf_op jit(solution)/shard_map/spread_last/pallas_call | solution.py:85
  560.7 4.3 copy.155
  572.6 5.2 copy.257
  577.9 5.3 copy.158
  586.4 3.8 convert_bitcast_fusion.1
  603.0 5.5 convolution_convert_fusion
  608.5 6.5 copy.171
  615.0 6.3 copy.172
  621.3 73.8 %dp_scatter.1 = (f32[2,128,256]{2,1,0:T(8,128)}, f32[2,9,128,256]{3,2,1,0:T(8,128)}, f32[2,128,64]{2,1,0:T(8,128)}, f32[2,64,128]{2,1,0:T(8,128)}, f32[2,128,256...) custom-call(bf16[4,2,128,256]{3,2,1,0:T(8,128)(2,1)} %maximum_bitcast_fusion.1.refs_0_, ...), custom_call_target="tpu_custom_call" | custom-call | tf_op jit(solution)/shard_map/dp_scatter/pallas_call | solution.py:231
  695.2 6.6 all-reduce.2
  (346 shorter events, 136.4 us)
Async XLA Ops:
  0.6 232.4 %copy-start = (bf16[1024,512]{1,0:T(8,128)(2,1)S(1)}, bf16[1024,512]{1,0:T(8,128)(2,1)}, u32[]{:S(2)}) copy-start(bf16[1024,512]{1,0:T(8,128)(2,1)} %param.26) | copy-start | bytes 3145732
  120.8 66.3 %copy-start.38 = (f32[1,8,128]{2,0,1:T(1,128)}, f32[1,8,128]{2,0,1:T(1,128)S(1)}, u32[]{:S(2)}) copy-start(f32[1,8,128]{2,0,1:T(1,128)S(1)} %get-tuple-element.135) | copy-start | bytes 12292
  120.9 66.3 %copy-start.45 = (f32[1,8,128]{2,0,1:T(1,128)}, f32[1,8,128]{2,0,1:T(1,128)S(1)}, u32[]{:S(2)}) copy-start(f32[1,8,128]{2,0,1:T(1,128)S(1)} %get-tuple-element.136) | copy-start | bytes 12292
  131.5 15.7 %copy-start.77 = (f32[2,128]{1,0:T(2,128)S(1)}, f32[2,128]{1,0:T(2,128)}, u32[]{:S(2)}) copy-start(f32[2,128]{1,0:T(2,128)} %param.24) | copy-start | bytes 3076
  131.5 16.2 %copy-start.24 = (bf16[2,128,256]{2,1,0:T(8,128)(2,1)S(1)}, bf16[2,128,256]{2,1,0:T(8,128)(2,1)}, u32[]{:S(2)}) copy-start(bf16[2,128,256]{2,1,0:T(8,128)(2,1)} %param.21) | copy-start | bytes 393220
  131.5 31.4 %copy-start.74 = (f32[2,256]{1,0:T(2,128)S(1)}, f32[2,256]{1,0:T(2,128)}, u32[]{:S(2)}) copy-start(f32[2,256]{1,0:T(2,128)} %param.22) | copy-start | bytes 6148
  131.5 32.0 %copy-start.32 = (bf16[2,256,128]{2,1,0:T(8,128)(2,1)S(1)}, bf16[2,256,128]{2,1,0:T(8,128)(2,1)}, u32[]{:S(2)}) copy-start(bf16[2,256,128]{2,1,0:T(8,128)(2,1)} %param.23) | copy-start | bytes 393220
  147.2 16.3 %copy-start.68 = (f32[2,128]{1,0:T(2,128)}, f32[2,128]{1,0:T(2,128)S(1)}, u32[]{:S(2)}) copy-start(f32[2,128]{1,0:T(2,128)S(1)} %get-tuple-element.119) | copy-start | bytes 3076
  147.2 33.5 %copy-start.9 = (f32[288,1024]{1,0:T(8,128)S(1)}, f32[288,1024]{1,0:T(8,128)}, u32[]{:S(2)}) copy-start(f32[288,1024]{1,0:T(8,128)} %div.116) | copy-start | bytes 3538948
  236.6 44.9 %copy-start.73 = (f32[512]{0:T(512)S(1)}, f32[512]{0:T(512)}, u32[]{:S(2)}) copy-start(f32[512]{0:T(512)} %param.29) | copy-start | bytes 6148
  292.4 57.8 %copy-start.84 = (f32[288,512]{1,0:T(8,128)S(1)}, f32[288,512]{1,0:T(8,128)}, u32[]{:S(2)}) copy-start(f32[288,512]{1,0:T(8,128)} %copy-done.83) | copy-start | bytes 1769476
  387.1 16.2 %copy-start.19 = (f32[2,12,12,128]{3,2,1,0:T(8,128)S(1)}, f32[2,12,12,128]{3,2,1,0:T(8,128)}, u32[]{:S(2)}) copy-start(f32[2,12,12,128]{3,2,1,0:T(8,128)} %copy.137) | copy-start | bytes 442372
  387.2 17.1 %copy-start.33 = (bf16[2,256,128]{2,1,0:T(8,128)(2,1)S(1)}, bf16[2,256,128]{2,1,0:T(8,128)(2,1)}, u32[]{:S(2)}) copy-start(bf16[2,256,128]{2,1,0:T(8,128)(2,1)} %param.23) | copy-start | bytes 393220
  387.2 17.1 %copy-start.50 = (f32[2,128]{1,0:T(2,128)S(1)}, f32[2,128]{1,0:T(2,128)}, u32[]{:S(2)}) copy-start(f32[2,128]{1,0:T(2,128)} %copy-done.49) | copy-start | bytes 3076
  387.2 25.8 %copy-start.58 = (f32[2,256]{1,0:T(2,128)S(1)}, f32[2,256]{1,0:T(2,128)}, u32[]{:S(2)}) copy-start(f32[2,256]{1,0:T(2,128)} %squeeze.47) | copy-start | bytes 6148
  387.2 25.8 %copy-start.65 = (f32[1,256]{1,0:T(1,128)S(1)}, f32[1,256]{1,0:T(1,128)}, u32[]{:S(2)}) copy-start(f32[1,256]{1,0:T(1,128)} %get-tuple-element.139) | copy-start | bytes 3076
  387.2 27.1 %copy-start.25 = (bf16[2,128,256]{2,1,0:T(8,128)(2,1)S(1)}, bf16[2,128,256]{2,1,0:T(8,128)(2,1)}, u32[]{:S(2)}) copy-start(bf16[2,128,256]{2,1,0:T(8,128)(2,1)} %param.21) | copy-start | bytes 393220
  404.3 13.1 %copy-start.16 = (bf16[1,128,9,1024]{3,1,2,0:T(8,128)(2,1)S(1)}, bf16[1,128,9,1024]{3,1,2,0:T(8,128)(2,1)}, u32[]{:S(2)}) copy-start(bf16[1,128,9,1024]{3,1,2,0:T(8,128)(2,1)} %get-tuple-element.121) | copy-start | bytes 7077892
  418.3 14.8 %copy-start.39 = (f32[1,8,128]{2,0,1:T(1,128)S(1)}, f32[1,8,128]{2,0,1:T(1,128)}, u32[]{:S(2)}) copy-start(f32[1,8,128]{2,0,1:T(1,128)} %copy-done.38) | copy-start | bytes 12292
  418.3 17.1 %copy-start.20 = (f32[36,1024]{1,0:T(8,128)S(1)}, f32[36,1024]{1,0:T(8,128)}, u32[]{:S(2)}) copy-start(f32[36,1024]{1,0:T(8,128)} %scatter_g.1) | copy-start | bytes 442372
  452.5 14.4 %copy-start.57 = (f32[2,256]{1,0:T(2,128)S(1)}, f32[2,256]{1,0:T(2,128)}, u32[]{:S(2)}) copy-start(f32[2,256]{1,0:T(2,128)} %squeeze.46) | copy-start | bytes 6148
  452.5 14.4 %copy-start.64 = (f32[1,256]{1,0:T(1,128)S(1)}, f32[1,256]{1,0:T(1,128)}, u32[]{:S(2)}) copy-start(f32[1,256]{1,0:T(1,128)} %copy-done.63) | copy-start | bytes 3076
  452.5 15.7 %copy-start.26 = (bf16[2,128,256]{2,1,0:T(8,128)(2,1)S(1)}, bf16[2,128,256]{2,1,0:T(8,128)(2,1)}, u32[]{:S(2)}) copy-start(bf16[2,128,256]{2,1,0:T(8,128)(2,1)} %param.21) | copy-start | bytes 393220
  525.1 34.4 %copy-start.14 = (f32[2,12,2,12,2,128]{5,4,3,2,1,0:T(2,128)S(1)}, f32[2,12,2,12,2,128]{5,4,3,2,1,0:T(2,128)}, u32[]{:S(2)}) copy-start(f32[2,12,2,12,2,128]{5,4,3,2,1,0:T(2,128)} %broadcast_in_dim.19) | copy-start | bytes 1769476
  525.2 35.2 %copy-start.29 = (bf16[8,36,128]{2,1,0:T(8,128)(2,1)S(1)}, bf16[8,36,128]{2,1,0:T(8,128)(2,1)}, u32[]{:S(2)}) copy-start(bf16[8,36,128]{2,1,0:T(8,128)(2,1)} %get-tuple-element.131) | copy-start | bytes 221188
  590.3 6.1 copy-start.27
  590.3 6.1 copy-start.13
  621.3 73.9 %copy-start.75 = (f32[4,128]{1,0:T(4,128)S(1)}, f32[4,128]{1,0:T(4,128)}, u32[]{:S(2)}) copy-start(f32[4,128]{1,0:T(4,128)} %get-tuple-element.30) | copy-start | bytes 6148
  621.3 73.9 %copy-start.71 = (f32[256]{0:T(256)S(1)}, f32[256]{0:T(256)}, u32[]{:S(2)}) copy-start(f32[256]{0:T(256)} %get-tuple-element.115) | copy-start | bytes 3076
  621.3 73.9 %copy-start.72 = (f32[256]{0:T(256)S(1)}, f32[256]{0:T(256)}, u32[]{:S(2)}) copy-start(f32[256]{0:T(256)} %get-tuple-element.113) | copy-start | bytes 3076
  621.3 74.0 %copy-start.67 = (f32[512]{0:T(512)S(1)}, f32[512]{0:T(512)}, u32[]{:S(2)}) copy-start(f32[512]{0:T(512)} %get-tuple-element.111) | copy-start | bytes 6148
  621.3 74.0 %copy-start.76 = (f32[512]{0:T(512)S(1)}, f32[512]{0:T(512)}, u32[]{:S(2)}) copy-start(f32[512]{0:T(512)} %get-tuple-element.152) | copy-start | bytes 6148
  (54 other events, 166.9 us)
